TPU v7x, 32 devices: a whole 2x2x4 slice. The times are simulated.
32 devices in a mesh: dp: 8 (over z, core), tensor: 4 (over y, x).
Axes of the slice: x: 2, y: 2, z: 4, core: 2. Of those that a mesh axis runs over, the one named last changes fastest.
Arguments:
- inputs: bfloat16 [8, 1024, 1024], P('dp'), may hold values from -6 to 6
- cotangent: bfloat16 [8, 1024, 1024], P('dp'), may hold values from -6 to 6
- groups: int32 [8], P('dp'), may hold values from 0 to 7
- counts: int32 [8], replicated, may hold values from 128 to 512
- vector_parameters: float32 [6, 1024], replicated, may hold values from -0.9 to 1.4, as said below
- query_value_bias: float32 [2, 1024], P(None, 'tensor'), may hold values from -1.8 to 1.8
- hidden_bias: float32 [4096], P('tensor'), may hold values from -1.8 to 1.8
- query_key_value_weight: bfloat16 [3, 1024, 1024], P(None, None, 'tensor'), may hold values from -0.1875 to 0.1875
- attention_output_weight: bfloat16 [1024, 1024], P('tensor'), may hold values from -0.75 to 0.75
- hidden_weight: bfloat16 [1024, 4096], P(None, 'tensor'), may hold values from -0.1875 to 0.1875
- hidden_output_weight: bfloat16 [4096, 1024], P('tensor'), may hold values from -0.09375 to 0.09375
- adapter_down: float32 [2, 1024, 4], replicated, may hold values from -0.1875 to 0.1875
- adapter_up: float32 [2, 4, 1024], replicated, may hold values from -0.18 to 0.18
- momentum_down: float32 [2, 1024, 4], replicated, may hold values from -0.039774757 to 0.039774757
- momentum_up: float32 [2, 4, 1024], replicated, may hold values from -0.079549514 to 0.079549514
- average_down: float32 [2, 1024, 4], replicated, may hold values from -0.1875 to 0.1875
- average_up: float32 [2, 4, 1024], replicated, may hold values from -0.18 to 0.18
Outputs:
- block_out: bfloat16 [8, 1024, 1024], P('dp')
- input_grad: bfloat16 [8, 1024, 1024], P('dp')
- down_gradient: float32 [2, 1024, 4], replicated
- up_gradient: float32 [2, 4, 1024], replicated
- updated_momentum_down: float32 [2, 1024, 4], replicated
- updated_momentum_up: float32 [2, 4, 1024], replicated
- updated_down: float32 [2, 1024, 4], replicated
- updated_up: float32 [2, 4, 1024], replicated
- updated_average_down: float32 [2, 1024, 4], replicated
- updated_average_up: float32 [2, 4, 1024], replicated
- copy_a: bfloat16 [2, 1024, 4], replicated
- copy_b: bfloat16 [2, 4, 1024], replicated
Inputs may be any that keep to these rules, and one draw needn't show every extreme that they name: `vector_parameters`: rows 0 and 2 are gains, the other rows shifts and biases.
All inputs are finite; a program needn't handle non-finite values.
Results may differ from a plain program's by a relative error of at most 0.018.
Values may be sent and summed in bfloat16 or wider, within the bound.
No kernel may reach another device: no remote copies, remote signals or barrier semaphores. Data moves between devices by JAX's collectives and lax.ppermute only.
A program may use at most 128 MiB of HBM per device.

v0:
```python
import math
import jax
import jax.numpy as jnp
from jax import lax
from jax.sharding import PartitionSpec as P

HEAD = 64
NORM_EPS = 1e-05
ADAPTER_SCALE = 8.0
MASK_FILL = -1e30
MOMENTUM_FACTOR = 0.9
AVERAGE_KEEP = 0.8
RATE_BASE = 0.025
WEIGHT_DECAY = 0.005
COUNT_BASE = 256.0


def layer_norm(value_rows, norm_gain, norm_bias):
    center = value_rows - jnp.mean(value_rows, axis=-1, keepdims=True)
    spread = jnp.mean(center * center, axis=-1, keepdims=True)
    return center * lax.rsqrt(spread + NORM_EPS) * norm_gain + norm_bias


def norm_back(value_rows, norm_gain, norm_bias, upstream):

    def local_norm(operand):
        return layer_norm(operand, norm_gain, norm_bias)

    _, backward_map = jax.vjp(local_norm, value_rows)
    return backward_map(upstream)[0]


def gelu_back(preact, upstream):

    def activate(operand):
        return jax.nn.gelu(operand, approximate=True)

    _, backward_map = jax.vjp(activate, preact)
    return backward_map(upstream)[0]


def to_heads(matrix, seq_count, length):
    return matrix.reshape(seq_count, length, -1, HEAD).transpose(0, 2, 1, 3)


def to_rows(tensor4):
    return tensor4.transpose(0, 2, 1, 3).reshape(-1, tensor4.shape[1] * tensor4.shape[3])


def block_scores(query_block, keys, offset, scale_att):
    scores = (
        jnp.einsum("shqe,shke->shqk", query_block, keys, preferred_element_type=jnp.float32)
        * scale_att
    )
    query_pos = offset + jnp.arange(query_block.shape[2])
    key_pos = jnp.arange(keys.shape[2])
    return jnp.where(key_pos[None, :] <= query_pos[:, None], scores, MASK_FILL)


def attend(query_rows, keys, value_rows, scale_att):
    length = query_rows.shape[2]
    block_len = min(512, length)
    outputs = []
    log_totals = []
    for offset in range(0, length, block_len):
        query_block = query_rows[:, :, offset : offset + block_len]
        scores = block_scores(query_block, keys, offset, scale_att)
        largest = jnp.max(scores, axis=-1, keepdims=True)
        exponent = jnp.exp(scores - largest)
        summed = jnp.sum(exponent, axis=-1, keepdims=True)
        attention = exponent / summed
        log_totals.append(largest + jnp.log(summed))
        outputs.append(
            jnp.einsum(
                "shqk,shke->shqe",
                attention.astype(jnp.bfloat16),
                value_rows,
                preferred_element_type=jnp.float32,
            )
        )
    return (jnp.concatenate(outputs, axis=2), log_totals)


def attend_back(query_rows, keys, value_rows, log_totals, grad_heads, scale_att):
    length = query_rows.shape[2]
    block_len = min(512, length)
    grad_blocks = []
    grad_keys = jnp.zeros(keys.shape, jnp.float32)
    grad_values = jnp.zeros(value_rows.shape, jnp.float32)
    for number, offset in enumerate(range(0, length, block_len)):
        query_block = query_rows[:, :, offset : offset + block_len]
        grad_block = grad_heads[:, :, offset : offset + block_len]
        scores = block_scores(query_block, keys, offset, scale_att)
        attention = jnp.exp(scores - log_totals[number])
        grad_attn = jnp.einsum(
            "shqe,shke->shqk", grad_block, value_rows, preferred_element_type=jnp.float32
        )
        row_inner = jnp.sum(grad_attn * attention, axis=-1, keepdims=True)
        grad_scores = (attention * (grad_attn - row_inner)).astype(jnp.bfloat16)
        grad_blocks.append(
            jnp.einsum("shqk,shke->shqe", grad_scores, keys, preferred_element_type=jnp.float32)
            * scale_att
        )
        grad_keys = (
            grad_keys
            + jnp.einsum(
                "shqk,shqe->shke", grad_scores, query_block, preferred_element_type=jnp.float32
            )
            * scale_att
        )
        grad_values = grad_values + jnp.einsum(
            "shqk,shqe->shke",
            attention.astype(jnp.bfloat16),
            grad_block,
            preferred_element_type=jnp.float32,
        )
    return (jnp.concatenate(grad_blocks, axis=2), grad_keys, grad_values)


def update_step(gradient_term, moment, weight_matrix, average, learning_rate):
    updated_moment = MOMENTUM_FACTOR * moment + gradient_term
    updated_weight = weight_matrix * (
        1.0 - learning_rate * WEIGHT_DECAY * ADAPTER_SCALE
    ) - learning_rate * (gradient_term + MOMENTUM_FACTOR * updated_moment)
    new_average = AVERAGE_KEEP * average + (1.0 - AVERAGE_KEEP) * updated_weight
    return (updated_moment, updated_weight, new_average)


def local(
    inputs,
    cotangent,
    groups,
    counts,
    vector_parameters,
    query_value_bias,
    hidden_bias,
    query_key_value_weight,
    attention_output_weight,
    hidden_weight,
    hidden_output_weight,
    adapter_down,
    adapter_up,
    momentum_down,
    momentum_up,
    average_down,
    average_up,
):
    seq_count, length, width_value = inputs.shape
    row_count = seq_count * length
    resid_in = inputs.reshape(row_count, width_value).astype(jnp.float32)
    first_norm_output = layer_norm(resid_in, vector_parameters[0], vector_parameters[1]).astype(
        jnp.bfloat16
    )
    local_width = query_key_value_weight.shape[2]
    column_start = lax.axis_index("tensor") * local_width
    down_reduced = adapter_down.astype(jnp.bfloat16)
    up_reduced = adapter_up.astype(jnp.bfloat16)
    up_local = lax.dynamic_slice_in_dim(up_reduced, column_start, local_width, 2)
    projected_rows = jnp.einsum(
        "rd,cde->cre", first_norm_output, query_key_value_weight, preferred_element_type=jnp.float32
    )
    adapter_input = jnp.einsum(
        "wo,qob->qwb", first_norm_output, down_reduced, preferred_element_type=jnp.float32
    ).astype(jnp.bfloat16)
    adapter_output = jnp.einsum(
        "iga,iaj->igj", adapter_input, up_local, preferred_element_type=jnp.float32
    )
    query_rows = (
        projected_rows[0] + query_value_bias[0] + ADAPTER_SCALE * adapter_output[0]
    ).astype(jnp.bfloat16)
    keys_low = projected_rows[1].astype(jnp.bfloat16)
    value_reduced = (
        projected_rows[2] + query_value_bias[1] + ADAPTER_SCALE * adapter_output[1]
    ).astype(jnp.bfloat16)
    scale_att = HEAD ** (-0.5)
    query_heads = to_heads(query_rows, seq_count, length)
    key_heads = to_heads(keys_low, seq_count, length)
    value_heads = to_heads(value_reduced, seq_count, length)
    heads_out, log_totals = attend(query_heads, key_heads, value_heads, scale_att)
    merged = to_rows(heads_out).astype(jnp.bfloat16)
    attn_part = jnp.dot(merged, attention_output_weight, preferred_element_type=jnp.float32)
    tile = row_count // lax.axis_size("tensor")
    row_offset = lax.axis_index("tensor") * tile
    one_hot = groups[:, None] == jnp.arange(counts.shape[0])[None, :]
    seq_counts = jnp.sum(jnp.where(one_hot, counts[None, :], 0), axis=1).astype(jnp.float32)
    seq_weight = COUNT_BASE / seq_counts
    grad_out = (cotangent.astype(jnp.float32) * seq_weight[:, None, None]).reshape(
        row_count, width_value
    )
    grad_low = grad_out.astype(jnp.bfloat16)
    attn_share = lax.psum_scatter(
        attn_part.astype(jnp.bfloat16), "tensor", scatter_dimension=0, tiled=True
    ).astype(jnp.float32)
    input_share = lax.dynamic_slice_in_dim(resid_in, row_offset, tile, 0)
    resid_share = input_share + attn_share + vector_parameters[4]
    norm_share = layer_norm(resid_share, vector_parameters[2], vector_parameters[3]).astype(
        jnp.bfloat16
    )
    norm2 = lax.all_gather(norm_share, "tensor", axis=0, tiled=True)
    preact = jnp.dot(norm2, hidden_weight, preferred_element_type=jnp.float32) + hidden_bias
    act_low = jax.nn.gelu(preact, approximate=True).astype(jnp.bfloat16)
    preact, mlp_part = (
        preact,
        jnp.dot(act_low, hidden_output_weight, preferred_element_type=jnp.float32),
    )
    mlp_share = lax.psum_scatter(
        mlp_part.astype(jnp.bfloat16), "tensor", scatter_dimension=0, tiled=True
    ).astype(jnp.float32)
    output_share = (resid_share + mlp_share + vector_parameters[5]).astype(jnp.bfloat16)
    output_rows = lax.all_gather(output_share, "tensor", axis=0, tiled=True)
    grad_act = jnp.einsum(
        "rd,fd->rf", grad_low, hidden_output_weight, preferred_element_type=jnp.float32
    )
    grad_pre = gelu_back(preact, grad_act).astype(jnp.bfloat16)
    grad_norm_share = lax.psum_scatter(
        jnp.einsum("rf,df->rd", grad_pre, hidden_weight, preferred_element_type=jnp.float32).astype(
            jnp.bfloat16
        ),
        "tensor",
        scatter_dimension=0,
        tiled=True,
    ).astype(jnp.float32)
    grad_out_share = lax.dynamic_slice_in_dim(grad_out, row_offset, tile, 0)
    grad_resid_share = grad_out_share + norm_back(
        resid_share, vector_parameters[2], vector_parameters[3], grad_norm_share
    )
    grad_resid_low = lax.all_gather(
        grad_resid_share.astype(jnp.bfloat16), "tensor", axis=0, tiled=True
    )
    grad_merged = jnp.einsum(
        "rd,ed->re", grad_resid_low, attention_output_weight, preferred_element_type=jnp.float32
    ).astype(jnp.bfloat16)
    grad_q, grad_k, grad_v = attend_back(
        query_heads,
        key_heads,
        value_heads,
        log_totals,
        to_heads(grad_merged, seq_count, length),
        scale_att,
    )
    grad_qkv = jnp.stack([to_rows(grad_q), to_rows(grad_k), to_rows(grad_v)]).astype(jnp.bfloat16)
    grad_norm1 = jnp.einsum(
        "cre,cde->rd", grad_qkv, query_key_value_weight, preferred_element_type=jnp.float32
    )
    query_value_gradient = jnp.stack([grad_qkv[0], grad_qkv[2]])
    adapter_input_gradient = ADAPTER_SCALE * jnp.einsum(
        "cre,cke->crk", query_value_gradient, up_local, preferred_element_type=jnp.float32
    )
    grad_norm1 = grad_norm1 + jnp.einsum(
        "ibp,inp->bn",
        adapter_input_gradient,
        down_reduced.astype(jnp.float32),
        precision=lax.Precision.HIGHEST,
    )
    grad_a_part = jnp.einsum(
        "rd,crk->cdk",
        first_norm_output,
        adapter_input_gradient,
        precision=lax.Precision.HIGHEST,
        preferred_element_type=jnp.float32,
    )
    local_up_gradient = ADAPTER_SCALE * jnp.einsum(
        "ipg,ipd->igd", adapter_input, query_value_gradient, preferred_element_type=jnp.float32
    )
    grad_b_part = lax.dynamic_update_slice(
        jnp.zeros((2, adapter_up.shape[1], width_value), jnp.float32),
        local_up_gradient,
        (0, 0, column_start),
    )
    grad_norm1_share = lax.psum_scatter(
        grad_norm1.astype(jnp.bfloat16), "tensor", scatter_dimension=0, tiled=True
    ).astype(jnp.float32)
    grad_input_share = grad_resid_share + norm_back(
        input_share, vector_parameters[0], vector_parameters[1], grad_norm1_share
    )
    grad_a_sum, grad_b_sum, weight_sum = lax.psum(
        (grad_a_part, grad_b_part, jnp.sum(seq_weight)), ("dp", "tensor")
    )
    mean_weight = weight_sum / (lax.axis_size("dp") * lax.axis_size("tensor") * seq_count)
    tokens_all = lax.axis_size("dp") * seq_count * length
    input_grad = lax.all_gather(
        (grad_input_share / mean_weight).astype(jnp.bfloat16), "tensor", axis=0, tiled=True
    )
    down_gradient = grad_a_sum / (mean_weight * tokens_all)
    up_gradient = grad_b_sum / (mean_weight * tokens_all)
    learning_rate = RATE_BASE * math.sqrt(tokens_all)
    updated_momentum_down, updated_down, updated_average_down = update_step(
        down_gradient, momentum_down, adapter_down, average_down, learning_rate
    )
    updated_momentum_up, updated_up, updated_average_up = update_step(
        up_gradient, momentum_up, adapter_up, average_up, learning_rate
    )
    block_out = output_rows.reshape(seq_count, length, width_value)
    input_grad = input_grad.reshape(seq_count, length, width_value)
    return (
        block_out,
        input_grad,
        down_gradient,
        up_gradient,
        updated_momentum_down,
        updated_momentum_up,
        updated_down,
        updated_up,
        updated_average_down,
        updated_average_up,
        updated_down.astype(jnp.bfloat16),
        updated_up.astype(jnp.bfloat16),
    )


def solution(mesh):
    in_specs = (
        P("dp", None, None),
        P("dp", None, None),
        P("dp"),
        P(),
        P(),
        P(None, "tensor"),
        P("tensor"),
        P(None, None, "tensor"),
        P("tensor", None),
        P(None, "tensor"),
        P("tensor", None),
        P(),
        P(),
        P(),
        P(),
        P(),
        P(),
    )
    out_specs = (
        P("dp", None, None),
        P("dp", None, None),
        P(),
        P(),
        P(),
        P(),
        P(),
        P(),
        P(),
        P(),
        P(),
        P(),
    )
    return jax.shard_map(local, mesh=mesh, in_specs=in_specs, out_specs=out_specs, check_vma=False)
```

profile of v0, /device:TPU:0, one launch (start us, length us, event | category | flops | bytes accessed | tf_op | source)
XLA Modules:
  0.0 417.0 jit_solution(1746353176748242203)
XLA Ops:
  7.3 0.9 iota_compare_fusion.1
  8.2 1.0 fusion.92
  9.2 1.9 convert_reduce_fusion
  11.2 2.3 multiply_reduce_fusion.2
  13.5 2.4 fusion.20
  15.9 1.3 copy-done.6
  17.2 0.6 fusion.51
  18.4 1.2 slice_multiply_fusion.1
  19.6 0.7 copy-done.35
  20.3 3.0 fusion.93
  23.3 1.6 fusion.90
  25.0 1.1 fusion.91
  26.1 0.8 pad_maximum_fusion.3
  26.9 2.2 reshape.355
  29.6 1.7 fusion.54
  31.4 3.2 fusion.94
  34.6 1.9 fusion.95
  36.6 1.9 fusion.1
  38.8 1.9 fusion.48
  40.7 1.7 fusion
  42.5 1.9 fusion.47
  44.5 2.1 convolution_convert_fusion.1
  46.6 4.0 convert_element_type.147
  50.6 34.0 %reduce-scatter.5.cloned.1.call-done = bf16[256,1024]{1,0:T(8,128)(2,1)} async-done(((bf16[1024,1024]{1,0:T(8,128)(2,1)}), bf16[256,1024]{1,0:T(8,128)(2,1)}) %reduce-scatter.5.cloned.1.call-update) | async-done | bytes 524304 | tf_op jit(solution)/shard_map/reduce_scatter | solution.py:191
  84.6 1.6 fusion.88
  86.5 1.1 add_convert_fusion.2
  89.6 33.3 %all-gather.5.cloned.1.call-done = bf16[1024,1024]{1,0:T(8,128)(2,1)} async-done(((bf16[256,1024]{1,0:T(8,128)(2,1)}), bf16[1024,1024]{1,0:T(8,128)(2,1)}) %all-gather.5.cloned.1.call-update) | async-done | bytes 2097168 | tf_op jit(solution)/shard_map/all_gather | solution.py:199
  122.9 5.9 %fusion.96 = f32[1024,1024]{1,0:T(8,128)} fusion(bf16[1024,1024]{1,0:T(8,128)(2,1)} %all-gather.5.cloned.1.call-done, bf16[1024,1024]{1,0:T(8,128)(2,1)S(1)} %copy-done), kind=kOutput, calls=%fused_computation.171 | convolution fusion | flops 2147483648 | bytes 8388608 | tf_op jit(solution)/shard_map/dot_general | solution.py:200
  128.8 9.5 %convolution_convert_fusion = bf16[1024,1024]{1,0:T(8,128)(2,1)} fusion(bf16[1024,1024]{1,0:T(8,128)(2,1)S(1)} %copy-done, f32[1024,1024]{1,0:T(8,128)} %fusion.96, bf16[1024,1024]{1,0:T(8,128)(2,1)} %param.27, f32[1024]{0:T(1024)S(1)} %copy-done.36, bf16[1,1024,1024]{2,1,0:T(8,128)(2,1)} %param.18, f32[]{:T(128)S(6)} %div.95), kind=kOutput, calls=%fused_computation.47 | convolution fusion | flops 4321181696 | bytes 12587012 | tf_op jit(solution)/shard_map/rf,df->rd/dot_general | solution.py:216
  138.3 7.1 %fusion.27 = bf16[1024,1024]{1,0:T(8,128)(2,1)} fusion(bf16[1024,1024]{1,0:T(8,128)(2,1)} %param.27, f32[1024,1024]{1,0:T(8,128)} %fusion.96, f32[1024]{0:T(1024)S(1)} %copy-done.36), kind=kOutput, calls=%fused_computation.46 | convolution fusion | flops 2159017984 | bytes 8392704 | tf_op jit(solution)/shard_map/dot_general | solution.py:204
  145.8 2.5 convert_multiply_fusion
  148.3 25.3 %reduce-scatter.9.cloned.1.call-done = bf16[256,1024]{1,0:T(8,128)(2,1)} async-done(((bf16[1024,1024]{1,0:T(8,128)(2,1)}), bf16[256,1024]{1,0:T(8,128)(2,1)}) %reduce-scatter.9.cloned.1.call-update) | async-done | bytes 524304 | tf_op jit(solution)/shard_map/reduce_scatter | solution.py:215
  173.6 1.3 multiply_reduce_fusion.5
  174.9 36.7 %reduce-scatter.7.cloned.1.call-done = bf16[256,1024]{1,0:T(8,128)(2,1)} async-done(((bf16[1024,1024]{1,0:T(8,128)(2,1)}), bf16[256,1024]{1,0:T(8,128)(2,1)}) %reduce-scatter.7.cloned.1.call-update) | async-done | bytes 524304 | tf_op jit(solution)/shard_map/reduce_scatter | solution.py:206
  211.7 2.4 fusion.87
  214.1 2.6 fusion.63
  216.7 35.2 %all-gather.9.cloned.1.call-done = bf16[1024,1024]{1,0:T(8,128)(2,1)} async-done(((bf16[256,1024]{1,0:T(8,128)(2,1)}), bf16[1024,1024]{1,0:T(8,128)(2,1)}) %all-gather.9.cloned.1.call-update) | async-done | bytes 2097168 | tf_op jit(solution)/shard_map/all_gather | solution.py:227
  252.0 2.5 convolution_convert_fusion.2
  254.5 5.0 %fusion.11 = f32[4,1024,64]{1,2,0:T(8,128)S(1)} fusion(f32[4,512,1024]{2,1,0:T(8,128)} %copy-done.2, f32[4,512]{1,0:T(4,128)S(1)} %log_add_fusion, bf16[1,4,1024,64]{2,3,1,0:T(8,128)(2,1)S(1)} %bitcast.159), kind=kOutput, calls=%fused_computation.25 | convolution fusion | flops 272629760 | bytes 9707520 | tf_op jit(solution)/shard_map/shqk,shqe->shke/dot_general | solution.py:111
  259.6 4.3 %multiply_reduce_fusion = (f32[4,512]{1,0:T(4,128)S(1)}, f32[4,512,1024]{2,1,0:T(8,128)}) fusion(f32[4,512,1024]{2,1,0:T(8,128)S(1)} %bitcast.151, f32[4,512]{1,0:T(4,128)S(1)} %log_add_fusion, bf16[4,1024,64]{1,2,0:T(8,128)(2,1)S(1)} %copy-done.12, bf16[1,4,1024,64]{2,3,1,0:T(8,128)(2,1)S(1)} %bitcast.160), kind=kOutput, calls=%fused_computation.1 | convolution fusion | flops 274724864 | bytes 17580032 | tf_op jit(solution)/shard_map/shqe,shke->shqk/dot_general | solution.py:95
  263.9 2.6 multiply_reduce_fusion.1
  266.5 1.7 multiply_convert_fusion.1
  268.3 1.4 fusion.46
  269.7 0.8 fusion.60
  270.6 1.7 fusion.37
  272.5 6.9 %multiply_convert_fusion = bf16[4,512,1024]{2,1,0:T(8,128)(2,1)S(1)} fusion(f32[4,512,1024]{2,1,0:T(8,128)} %get-tuple-element.55, f32[4,512,1024]{2,1,0:T(8,128)} %copy-done.2, f32[4,512]{1,0:T(4,128)S(1)} %get-tuple-element.54, f32[4,512]{1,0:T(4,128)S(1)} %log_add_fusion), kind=kLoop, calls=%fused_computation | loop fusion | flops 8388608 | bytes 20987904 | tf_op jit(solution)/shard_map/convert_element_type | solution.py:99
  279.5 1.9 copy-done.4
  281.4 1.4 fusion.45
  283.5 3.8 fusion.64
  287.4 0.9 fusion.40
  288.5 5.8 %fusion.15 = bf16[1024,1024]{1,0:T(8,128)(2,1)} fusion(f32[1024,1024,1]{1,0,2:T(8,128)} %fusion.64, bf16[3,1024,256]{2,1,0:T(8,128)(2,1)} %param.24, bf16[1,1024,256]{2,1,0:T(8,128)(2,1)S(1)} %copy.36, bf16[1,1024,256]{2,1,0:T(8,128)(2,1)S(1)} %copy.35, bf16[1,1024,256]{2,1,0:T(8,128)(2,1)S(1)} %copy.34), kind=kOutput, calls=%fused_computation.28 | convolution fusion | flops 1614282752 | bytes 9437184 | tf_op jit(solution)/shard_map/cre,cde->rd/dot_general | solution.py:242
  294.4 0.7 all-gather.7.cloned.1.call-update
  295.4 1.4 dynamic-slice_reduce_fusion
  296.8 1.5 fusion.52
  298.2 1.0 convolution_bitcast_fusion.1
  299.3 40.8 %all-reduce.2 = (f32[]{:T(128)}, f32[2,1024,4]{1,2,0:T(4,128)S(1)}, f32[2,4,1024]{2,1,0:T(4,128)S(1)}) all-reduce(f32[]{:T(128)S(6)} %div.95, f32[2,1024,4]{1,2,0:T(4,128)S(1)} %convolution_bitcast_fusion.1, f32[2,4,1024]{2,1,0:T(4,128)S(1)} %fusion.52), channel_id=1, replica_groups=mesh['dp'=8,'tensor'=4] {'dp','tensor'}, use_global_device_ids=true, to_apply=%region_21.22 | all-reduce | flops 16385 | bytes 131080 | tf_op jit(solution)/shard_map/psum | solution.py:276
  340.7 1.8 multiply_reduce_fusion.4
  342.5 1.8 fusion.84
  344.3 3.0 divide_convert_fusion.12
  348.0 19.5 %all-gather.7.cloned.1.call-done = bf16[1024,1024]{1,0:T(8,128)(2,1)} async-done(((bf16[256,1024]{1,0:T(8,128)(2,1)}), bf16[1024,1024]{1,0:T(8,128)(2,1)}) %all-gather.7.cloned.1.call-update) | async-done | bytes 2097168 | tf_op jit(solution)/shard_map/all_gather | solution.py:210
  368.8 0.6 fusion.85
  370.1 35.1 %all-gather.11.cloned.1.call-done = bf16[1024,1024]{1,0:T(8,128)(2,1)} async-done(((bf16[256,1024]{1,0:T(8,128)(2,1)}), bf16[1024,1024]{1,0:T(8,128)(2,1)}) %all-gather.11.cloned.1.call-update) | async-done | bytes 2097168 | tf_op jit(solution)/shard_map/all_gather | solution.py:281
  405.1 3.2 copy.59
  408.4 1.3 copy.60
  (129 shorter events, 6.4 us)
Async XLA Ops:
  7.2 115.7 %copy-start = (bf16[1024,1024]{1,0:T(8,128)(2,1)S(1)}, bf16[1024,1024]{1,0:T(8,128)(2,1)}, u32[]{:S(2)}) copy-start(bf16[1024,1024]{1,0:T(8,128)(2,1)} %param.26) | copy-start | bytes 6291460
  7.2 77.5 %reduce-scatter.5.cloned.1.call-start = ((), (), s32[]{:S(2)}) async-start(), calls=%async_computation.4 | async-start | bytes 2621440 | tf_op jit(solution)/shard_map/reduce_scatter | solution.py:191
  9.2 8.0 %copy-start.26 = (f32[2,1024,4]{1,2,0:T(4,128)S(1)}, f32[2,1024,4]{1,2,0:T(4,128)}, u32[]{:S(2)}) copy-start(f32[2,1024,4]{1,2,0:T(4,128)} %param.28) | copy-start | bytes 98308
  11.1 6.7 %copy-start.29 = (f32[2,4,1024]{2,1,0:T(4,128)S(1)}, f32[2,4,1024]{2,1,0:T(4,128)}, u32[]{:S(2)}) copy-start(f32[2,4,1024]{2,1,0:T(4,128)} %param.29) | copy-start | bytes 98308
  15.9 1.3 copy-start.6
  17.9 1.7 copy-start.7
  17.9 2.4 copy-start.35
  23.3 1.6 copy-start.34
  31.3 3.2 copy-start.14
  31.3 3.2 copy-start.18
  31.4 3.2 copy-start.21
  34.6 4.2 copy-start.2
  36.5 5.9 %copy-start.3 = (f32[4,512,1024]{2,1,0:T(8,128)}, f32[4,512,1024]{2,1,0:T(8,128)S(1)}, u32[]{:S(2)}) copy-start(f32[4,512,1024]{2,1,0:T(8,128)S(1)} %get-tuple-element.53) | copy-start | bytes 25165828
  36.6 2.0 copy-start.13
  38.8 3.7 copy-start.11
  42.5 2.0 copy-start.24
  46.6 76.3 %all-gather.5.cloned.1.call-start = ((), (), s32[]{:S(2)}) async-start(), calls=%async_computation.5 | async-start | bytes 2621440 | tf_op jit(solution)/shard_map/all_gather | solution.py:199
  50.6 37.7 %copy-start.37 = (s32[8]{0:T(128)S(1)}, s32[8]{0:T(128)}, u32[]{:S(2)}) copy-start(s32[8]{0:T(128)} %param.20) | copy-start | bytes 100
  87.6 86.0 %reduce-scatter.9.cloned.1.call-start = ((), (), s32[]{:S(2)}) async-start(), calls=%async_computation.8 | async-start | bytes 2621440 | tf_op jit(solution)/shard_map/reduce_scatter | solution.py:215
  89.6 39.2 %copy-start.36 = (f32[1024]{0:T(1024)S(1)}, f32[1024]{0:T(1024)}, u32[]{:S(2)}) copy-start(f32[1024]{0:T(1024)} %param.23) | copy-start | bytes 12292
  138.3 7.5 %copy-start.16 = (bf16[1,1024,1024]{2,1,0:T(8,128)(2,1)S(1)}, bf16[1,1024,1024]{2,1,0:T(8,128)(2,1)}, u32[]{:S(2)}) copy-start(bf16[1,1024,1024]{2,1,0:T(8,128)(2,1)} %param.18) | copy-start | bytes 6291460
  138.3 73.4 %reduce-scatter.7.cloned.1.call-start = ((), (), s32[]{:S(2)}) async-start(), calls=%async_computation.6 | async-start | bytes 2621440 | tf_op jit(solution)/shard_map/reduce_scatter | solution.py:206
  145.5 106.5 %all-gather.9.cloned.1.call-start = ((), (), s32[]{:S(2)}) async-start(), calls=%async_computation.9 | async-start | bytes 2621440 | tf_op jit(solution)/shard_map/all_gather | solution.py:227
  148.3 103.7 %copy-start.25 = (bf16[256,1024]{1,0:T(8,128)(2,1)S(1)}, bf16[256,1024]{1,0:T(8,128)(2,1)}, u32[]{:S(2)}) copy-start(bf16[256,1024]{1,0:T(8,128)(2,1)} %param.25) | copy-start | bytes 1572868
  214.1 40.4 %copy-start.9 = (f32[256,1024]{1,0:T(8,128)}, f32[256,1024]{1,0:T(8,128)S(1)}, u32[]{:S(2)}) copy-start(f32[256,1024]{1,0:T(8,128)S(1)} %get-tuple-element.28) | copy-start | bytes 3145732
  216.7 124.1 %reduce-scatter.11.cloned.1.call-start = ((), (), s32[]{:S(2)}) async-start(), calls=%async_computation.10 | async-start | bytes 2621440 | tf_op jit(solution)/shard_map/reduce_scatter | solution.py:270
  252.0 7.5 %slice-start = ((s8[8388608]{0:T(1024)(128)(4,1)}), s8[4194304]{0:T(1024)(128)(4,1)S(1)}, s32[]{:S(2)}) async-start(s8[8388608]{0:T(1024)(128)(4,1)} %bitcast.150), calls=%async_computation.12 | async-start | bytes 8388608
  254.5 5.0 %slice-start.1 = ((s8[8388608]{0:T(1024)(128)(4,1)}), s8[4194304]{0:T(1024)(128)(4,1)S(1)}, s32[]{:S(2)}) async-start(s8[8388608]{0:T(1024)(128)(4,1)} %bitcast.150), calls=%async_computation.13 | async-start | bytes 8388608
  254.5 5.0 %copy-start.12 = (bf16[4,1024,64]{1,2,0:T(8,128)(2,1)S(1)}, bf16[4,1024,64]{1,2,0:T(8,128)(2,1)}, u32[]{:S(2)}) copy-start(bf16[4,1024,64]{1,2,0:T(8,128)(2,1)} %copy-done.11) | copy-start | bytes 1572868
  254.5 9.4 %slice-start.2 = ((s8[8388608]{0:T(1024)(128)(4,1)}), s8[4194304]{0:T(1024)(128)(4,1)S(1)}, s32[]{:S(2)}) async-start(s8[8388608]{0:T(1024)(128)(4,1)} %bitcast.152), calls=%async_computation.14 | async-start | bytes 8388608
  259.5 4.3 %slice-start.3 = ((s8[8388608]{0:T(1024)(128)(4,1)}), s8[4194304]{0:T(1024)(128)(4,1)S(1)}, s32[]{:S(2)}) async-start(s8[8388608]{0:T(1024)(128)(4,1)} %bitcast.152), calls=%async_computation.15 | async-start | bytes 8388608
  266.5 1.8 copy-start.19
  268.2 1.5 copy-start.15
  272.5 16.0 %copy-start.22 = (bf16[1,1024,256]{2,1,0:T(8,128)(2,1)}, bf16[1,1024,256]{2,1,0:T(8,128)(2,1)S(1)}, u32[]{:S(2)}) copy-start(bf16[1,1024,256]{2,1,0:T(8,128)(2,1)S(1)} %copy.36) | copy-start | bytes 1572868
  272.5 8.9 %copy-start.20 = (bf16[4,1024,64]{1,0,2:T(4,128)(2,1)S(1)}, bf16[4,1024,64]{1,0,2:T(4,128)(2,1)}, u32[]{:S(2)}) copy-start(bf16[4,1024,64]{1,0,2:T(4,128)(2,1)} %reshape.355) | copy-start | bytes 1572868
  279.5 2.0 copy-start.4
  283.1 5.3 %copy-start.23 = (bf16[1,1024,256]{2,1,0:T(8,128)(2,1)}, bf16[1,1024,256]{2,1,0:T(8,128)(2,1)S(1)}, u32[]{:S(2)}) copy-start(bf16[1,1024,256]{2,1,0:T(8,128)(2,1)S(1)} %copy.34) | copy-start | bytes 1572868
  283.1 4.2 %copy-start.5 = (bf16[4,512,1024]{2,1,0:T(8,128)(2,1)S(1)}, bf16[4,512,1024]{2,1,0:T(8,128)(2,1)}, u32[]{:S(2)}) copy-start(bf16[4,512,1024]{2,1,0:T(8,128)(2,1)} %copy-done.4) | copy-start | bytes 12582916
  294.3 3.9 copy-start.8
  294.3 73.2 %all-gather.7.cloned.1.call-start = ((), (), s32[]{:S(2)}) async-start(), calls=%async_computation.7 | async-start | bytes 2621440 | tf_op jit(solution)/shard_map/all_gather | solution.py:210
  294.4 49.9 %copy-start.10 = (f32[256,1024]{1,0:T(8,128)S(1)}, f32[256,1024]{1,0:T(8,128)}, u32[]{:S(2)}) copy-start(f32[256,1024]{1,0:T(8,128)} %copy-done.9) | copy-start | bytes 3145732
  295.1 110.0 %all-gather.11.cloned.1.call-start = ((), (), s32[]{:S(2)}) async-start(), calls=%async_computation.11 | async-start | bytes 2621440 | tf_op jit(solution)/shard_map/all_gather | solution.py:281
  299.2 68.3 %copy-start.32 = (f32[2,1024,4]{1,2,0:T(4,128)S(1)}, f32[2,1024,4]{1,2,0:T(4,128)}, u32[]{:S(2)}) copy-start(f32[2,1024,4]{1,2,0:T(4,128)} %param.30) | copy-start | bytes 98308
  299.2 68.9 %copy-start.30 = (f32[2,1024,4]{1,2,0:T(4,128)S(1)}, f32[2,1024,4]{1,2,0:T(4,128)}, u32[]{:S(2)}) copy-start(f32[2,1024,4]{1,2,0:T(4,128)} %param.32) | copy-start | bytes 98308
  299.2 69.6 %copy-start.33 = (f32[2,4,1024]{2,1,0:T(4,128)S(1)}, f32[2,4,1024]{2,1,0:T(4,128)}, u32[]{:S(2)}) copy-start(f32[2,4,1024]{2,1,0:T(4,128)} %param.31) | copy-start | bytes 98308
  340.7 28.7 %copy-start.31 = (f32[2,4,1024]{2,1,0:T(4,128)S(1)}, f32[2,4,1024]{2,1,0:T(4,128)}, u32[]{:S(2)}) copy-start(f32[2,4,1024]{2,1,0:T(4,128)} %param.33) | copy-start | bytes 98308
  368.2 41.5 %copy-start.27 = (f32[2,1024,4]{1,2,0:T(4,128)}, f32[2,1024,4]{1,2,0:T(4,128)S(1)}, u32[]{:S(2)}) copy-start(f32[2,1024,4]{1,2,0:T(4,128)S(1)} %get-tuple-element.76) | copy-start | bytes 98308
  369.4 40.3 %copy-start.28 = (f32[2,4,1024]{2,1,0:T(4,128)}, f32[2,4,1024]{2,1,0:T(4,128)S(1)}, u32[]{:S(2)}) copy-start(f32[2,4,1024]{2,1,0:T(4,128)S(1)} %get-tuple-element.77) | copy-start | bytes 98308
  405.1 3.2 copy-start.17
  405.1 4.6 %copy-start.1 = (bf16[1024,1024]{1,0:T(8,128)(2,1)S(1)}, bf16[1024,1024]{1,0:T(8,128)(2,1)}, u32[]{:S(2)}) copy-start(bf16[1024,1024]{1,0:T(8,128)(2,1)} %param.26) | copy-start | bytes 6291460
Sparse Core Ops, SparseCore 0:
  46.7 37.9 reduce-scatter.4
  87.7 35.1 all-gather.4
  138.4 35.1 reduce-scatter.8
  176.4 35.1 reduce-scatter.6
  216.8 35.1 all-gather.8
  294.5 35.9 reduce-scatter.10
  332.3 35.1 all-gather.6
  369.9 35.1 all-gather.10
where the time goes:
time: 425 us; the launch traced here: 417 us
  waiting for transfers between devices  220 us (52%)
  matrix products  70.9 us (17%)
  other arithmetic  51.1 us (12%)
  blocking collectives  40.8 us (10%)
  between operations  17.9 us (4%)
  local copies, waits for them, and re-layouts  15.6 us (4%)
    psum x1, blocking collectives, local(): lax.psum((grad_a_part, grad_b_part, jnp.sum(seq_weight)), ('dp', 'tensor'))  40.8 us
    reduce_scatter x1, waiting for transfers between devices, local(): lax.psum_scatter(mlp_part.astype(jnp.bfloat16), 'tensor', scatter_dimensi...  36.7 us
    all_gather x1, waiting for transfers between devices, local(): lax.all_gather(grad_resid_share.astype(jnp.bfloat16), 'tensor', axis=0, t...  35.2 us
    all_gather x1, waiting for transfers between devices, local(): lax.all_gather((grad_input_share / mean_weight).astype(jnp.bfloat16), 'te...  35.1 us
    reduce_scatter x1, waiting for transfers between devices, local(): lax.psum_scatter(attn_part.astype(jnp.bfloat16), 'tensor', scatter_dimens...  34 us
    all_gather x1, waiting for transfers between devices, local(): norm2 = lax.all_gather(norm_share, 'tensor', axis=0, tiled=True)  33.3 us
    reduce_scatter x1, waiting for transfers between devices, local(): lax.psum_scatter(jnp.einsum('rf,df->rd', grad_pre, hidden_weight, preferr...  25.3 us
    all_gather x1, waiting for transfers between devices, local(): output_rows = lax.all_gather(output_share, 'tensor', axis=0, tiled=True)  19.5 us
  transfers between devices with their start and end apart: 8, of which 7 were waited for; matrix products, arithmetic and copies ran while one was open for 7% of the time, Pallas kernels for 0%

commit v1 on v0

--- a/solution.py
+++ b/solution.py
@@ -13,6 +13,16 @@
 RATE_BASE = 0.025
 WEIGHT_DECAY = 0.005
 COUNT_BASE = 256.0
+
+
+def ring_gather(x, axis, dim):
+    ways, here, step = (lax.axis_size(axis), lax.axis_index(axis), x.shape[dim])
+    shape = [n * ways if d == dim else n for d, n in enumerate(x.shape)]
+    full = lax.dynamic_update_slice_in_dim(jnp.zeros(shape, x.dtype), x, here * step, axis=dim)
+    for far in range(1, ways):
+        x = lax.ppermute(x, axis, [(d, (d + 1) % ways) for d in range(ways)])
+        full = lax.dynamic_update_slice_in_dim(full, x, (here - far) % ways * step, axis=dim)
+    return full
 
 
 def layer_norm(value_rows, norm_gain, norm_bias):
@@ -224,9 +234,7 @@
     grad_resid_share = grad_out_share + norm_back(
         resid_share, vector_parameters[2], vector_parameters[3], grad_norm_share
     )
-    grad_resid_low = lax.all_gather(
-        grad_resid_share.astype(jnp.bfloat16), "tensor", axis=0, tiled=True
-    )
+    grad_resid_low = ring_gather(grad_resid_share.astype(jnp.bfloat16), "tensor", 0)
     grad_merged = jnp.einsum(
         "rd,ed->re", grad_resid_low, attention_output_weight, preferred_element_type=jnp.float32
     ).astype(jnp.bfloat16)

time: 425 us -> 432 us (1.016)
    ppermute x0 -> x3, waiting for transfers between devices: none -> 36.8 us  [ring_gather(): x = lax.ppermute(x, axis, [(d, (d + 1) % ways) for d in range(ways)])]
    all_gather x1 -> x0, waiting for transfers between devices: 35.2 us -> none  [local(): lax.all_gather(grad_resid_share.astype(jnp.bfloat16), 'tensor', axis=0, t...]
  transfers between devices with their start and end apart: 8 -> 10, of which waited for: 7 -> 9; matrix products, arithmetic and copies ran while one was open for 7% -> 7% of each run, Pallas kernels for 0% -> 0%
where the time goes in v1:
time: 432 us; the launch traced here: 424 us
  waiting for transfers between devices  221 us (51%)
  matrix products  70.9 us (16%)
  other arithmetic  50.8 us (12%)
  blocking collectives  40.7 us (9%)
  local copies, waits for them, and re-layouts  19.7 us (5%)
  between operations  18 us (4%)
    psum x1, blocking collectives, local(): lax.psum((grad_a_part, grad_b_part, jnp.sum(seq_weight)), ('dp', 'tensor'))  40.7 us
    all_gather x1, waiting for transfers between devices, local(): lax.all_gather((grad_input_share / mean_weight).astype(jnp.bfloat16), 'te...  37.6 us
    ppermute x3, waiting for transfers between devices, ring_gather(): x = lax.ppermute(x, axis, [(d, (d + 1) % ways) for d in range(ways)])  36.8 us
    reduce_scatter x1, waiting for transfers between devices, local(): lax.psum_scatter(mlp_part.astype(jnp.bfloat16), 'tensor', scatter_dimensi...  36.7 us
    reduce_scatter x1, waiting for transfers between devices, local(): lax.psum_scatter(attn_part.astype(jnp.bfloat16), 'tensor', scatter_dimens...  34 us
    all_gather x1, waiting for transfers between devices, local(): norm2 = lax.all_gather(norm_share, 'tensor', axis=0, tiled=True)  33.3 us
    reduce_scatter x1, waiting for transfers between devices, local(): lax.psum_scatter(jnp.einsum('rf,df->rd', grad_pre, hidden_weight, preferr...  25.3 us
    all_gather x1, waiting for transfers between devices, local(): output_rows = lax.all_gather(output_share, 'tensor', axis=0, tiled=True)  17.1 us
  transfers between devices with their start and end apart: 10, of which 9 were waited for; matrix products, arithmetic and copies ran while one was open for 7% of the time, Pallas kernels for 0%

profile of v1, /device:TPU:0, one launch (start us, length us, event | category | flops | bytes accessed | tf_op | source)
XLA Modules:
  0.0 424.3 jit_solution(502023811518149708)
XLA Ops:
  7.3 0.9 iota_compare_fusion.1
  8.2 1.0 fusion.93
  9.2 1.9 convert_reduce_fusion
  11.2 2.3 multiply_reduce_fusion.2
  13.5 2.4 fusion.20
  15.9 1.3 copy-done.6
  18.4 1.2 slice_multiply_fusion.1
  20.3 3.0 fusion.94
  23.3 1.6 fusion.91
  25.0 1.1 fusion.92
  27.0 2.2 reshape.355
  29.7 1.7 fusion.54
  31.4 3.2 fusion.95
  34.6 1.9 fusion.96
  36.6 1.9 fusion.1
  38.8 1.9 fusion.48
  40.7 1.7 fusion
  42.5 1.9 fusion.47
  44.5 2.1 convolution_convert_fusion.1
  46.6 4.0 convert_element_type.147
  50.7 34.0 %reduce-scatter.5.cloned.1.call-done = bf16[256,1024]{1,0:T(8,128)(2,1)} async-done(((bf16[1024,1024]{1,0:T(8,128)(2,1)}), bf16[256,1024]{1,0:T(8,128)(2,1)}) %reduce-scatter.5.cloned.1.call-update) | async-done | bytes 524304 | tf_op jit(solution)/shard_map/reduce_scatter | solution.py:201
  84.7 1.6 fusion.89
  86.6 1.1 add_convert_fusion.2
  89.7 33.3 %all-gather.4.cloned.1.call-done = bf16[1024,1024]{1,0:T(8,128)(2,1)} async-done(((bf16[256,1024]{1,0:T(8,128)(2,1)}), bf16[1024,1024]{1,0:T(8,128)(2,1)}) %all-gather.4.cloned.1.call-update) | async-done | bytes 2097168 | tf_op jit(solution)/shard_map/all_gather | solution.py:209
  122.9 5.9 %fusion.97 = f32[1024,1024]{1,0:T(8,128)} fusion(bf16[1024,1024]{1,0:T(8,128)(2,1)} %all-gather.4.cloned.1.call-done, bf16[1024,1024]{1,0:T(8,128)(2,1)S(1)} %copy-done), kind=kOutput, calls=%fused_computation.175 | convolution fusion | flops 2147483648 | bytes 8388608 | tf_op jit(solution)/shard_map/dot_general | solution.py:210
  128.8 9.4 %convolution_convert_fusion = bf16[1024,1024]{1,0:T(8,128)(2,1)} fusion(bf16[1024,1024]{1,0:T(8,128)(2,1)S(1)} %copy-done, f32[1024,1024]{1,0:T(8,128)} %fusion.97, bf16[1024,1024]{1,0:T(8,128)(2,1)} %param.27, f32[1024]{0:T(1024)S(1)} %copy-done.36, bf16[1,1024,1024]{2,1,0:T(8,128)(2,1)} %param.18, f32[]{:T(128)S(6)} %div.95), kind=kOutput, calls=%fused_computation.47 | convolution fusion | flops 4321181696 | bytes 12587012 | tf_op jit(solution)/shard_map/rf,df->rd/dot_general | solution.py:226
  138.3 7.1 %fusion.27 = bf16[1024,1024]{1,0:T(8,128)(2,1)} fusion(bf16[1024,1024]{1,0:T(8,128)(2,1)} %param.27, f32[1024,1024]{1,0:T(8,128)} %fusion.97, f32[1024]{0:T(1024)S(1)} %copy-done.36), kind=kOutput, calls=%fused_computation.46 | convolution fusion | flops 2159017984 | bytes 8392704 | tf_op jit(solution)/shard_map/dot_general | solution.py:214
  145.8 2.5 convert_multiply_fusion
  148.3 25.3 %reduce-scatter.9.cloned.1.call-done = bf16[256,1024]{1,0:T(8,128)(2,1)} async-done(((bf16[1024,1024]{1,0:T(8,128)(2,1)}), bf16[256,1024]{1,0:T(8,128)(2,1)}) %reduce-scatter.9.cloned.1.call-update) | async-done | bytes 524304 | tf_op jit(solution)/shard_map/reduce_scatter | solution.py:225
  173.7 1.3 multiply_reduce_fusion.5
  175.0 36.7 %reduce-scatter.7.cloned.1.call-done = bf16[256,1024]{1,0:T(8,128)(2,1)} async-done(((bf16[1024,1024]{1,0:T(8,128)(2,1)}), bf16[256,1024]{1,0:T(8,128)(2,1)}) %reduce-scatter.7.cloned.1.call-update) | async-done | bytes 524304 | tf_op jit(solution)/shard_map/reduce_scatter | solution.py:216
  211.7 2.4 fusion.88
  214.1 1.6 broadcast_in_dim.38
  215.7 2.2 constant_dynamic-update-slice_fusion.3
  217.9 1.4 collective-permute-start
  219.4 12.9 %collective-permute-done = bf16[256,1024]{1,0:T(8,128)(2,1)S(1)} collective-permute-done((bf16[256,1024]{1,0:T(8,128)(2,1)S(1)}, bf16[256,1024]{1,0:T(8,128)(2,1)S(1)}, u32[]{:S(2)}, u32[]{:S(2)}) %collective-permute-start) | collective-permute-done | bytes 524320 | tf_op jit(solution)/shard_map/ppermute | solution.py:23
  232.9 13.0 %collective-permute-done.1 = bf16[256,1024]{1,0:T(8,128)(2,1)S(1)} collective-permute-done((bf16[256,1024]{1,0:T(8,128)(2,1)S(1)}, bf16[256,1024]{1,0:T(8,128)(2,1)S(1)}, u32[]{:S(2)}, u32[]{:S(2)}) %collective-permute-start.1) | collective-permute-done | bytes 524320 | tf_op jit(solution)/shard_map/ppermute | solution.py:23
  245.9 0.8 constant_dynamic-update-slice_fusion.2
  247.6 10.9 %collective-permute-done.2 = bf16[256,1024]{1,0:T(8,128)(2,1)S(1)} collective-permute-done((bf16[256,1024]{1,0:T(8,128)(2,1)S(1)}, bf16[256,1024]{1,0:T(8,128)(2,1)S(1)}, u32[]{:S(2)}, u32[]{:S(2)}) %collective-permute-start.2) | collective-permute-done | bytes 524320 | tf_op jit(solution)/shard_map/ppermute | solution.py:23
  259.3 2.5 convolution_convert_fusion.2
  261.9 5.0 %fusion.11 = f32[4,1024,64]{1,2,0:T(8,128)S(1)} fusion(f32[4,512,1024]{2,1,0:T(8,128)} %copy-done.2, f32[4,512]{1,0:T(4,128)S(1)} %log_add_fusion, bf16[1,4,1024,64]{2,3,1,0:T(8,128)(2,1)S(1)} %bitcast.160), kind=kOutput, calls=%fused_computation.25 | convolution fusion | flops 272629760 | bytes 9707520 | tf_op jit(solution)/shard_map/shqk,shqe->shke/dot_general | solution.py:121
  266.9 4.3 %multiply_reduce_fusion = (f32[4,512]{1,0:T(4,128)S(1)}, f32[4,512,1024]{2,1,0:T(8,128)}) fusion(f32[4,512,1024]{2,1,0:T(8,128)S(1)} %bitcast.152, f32[4,512]{1,0:T(4,128)S(1)} %log_add_fusion, bf16[4,1024,64]{1,2,0:T(8,128)(2,1)S(1)} %copy-done.12, bf16[1,4,1024,64]{2,3,1,0:T(8,128)(2,1)S(1)} %bitcast.161), kind=kOutput, calls=%fused_computation.1 | convolution fusion | flops 274724864 | bytes 17580032 | tf_op jit(solution)/shard_map/shqe,shke->shqk/dot_general | solution.py:105
  271.2 2.6 multiply_reduce_fusion.1
  273.8 1.7 multiply_convert_fusion.1
  275.6 1.4 fusion.46
  277.1 0.8 fusion.60
  277.9 1.7 fusion.37
  279.9 6.9 %multiply_convert_fusion = bf16[4,512,1024]{2,1,0:T(8,128)(2,1)S(1)} fusion(f32[4,512,1024]{2,1,0:T(8,128)} %get-tuple-element.57, f32[4,512,1024]{2,1,0:T(8,128)} %copy-done.2, f32[4,512]{1,0:T(4,128)S(1)} %get-tuple-element.56, f32[4,512]{1,0:T(4,128)S(1)} %log_add_fusion), kind=kLoop, calls=%fused_computation | loop fusion | flops 8388608 | bytes 20987904 | tf_op jit(solution)/shard_map/convert_element_type | solution.py:109
  286.8 2.0 copy-done.4
  288.8 1.4 fusion.45
  290.9 3.9 fusion.64
  294.7 0.9 fusion.40
  295.9 5.8 %fusion.15 = bf16[1024,1024]{1,0:T(8,128)(2,1)} fusion(f32[1024,1024,1]{1,0,2:T(8,128)} %fusion.64, bf16[3,1024,256]{2,1,0:T(8,128)(2,1)} %param.24, bf16[1,1024,256]{2,1,0:T(8,128)(2,1)S(1)} %copy.36, bf16[1,1024,256]{2,1,0:T(8,128)(2,1)S(1)} %copy.35, bf16[1,1024,256]{2,1,0:T(8,128)(2,1)S(1)} %copy.34), kind=kOutput, calls=%fused_computation.28 | convolution fusion | flops 1614282752 | bytes 9437184 | tf_op jit(solution)/shard_map/cre,cde->rd/dot_general | solution.py:250
  302.6 1.4 dynamic-slice_reduce_fusion
  304.0 1.5 fusion.52
  305.5 1.0 convolution_bitcast_fusion.1
  306.5 40.7 %all-reduce.2 = (f32[]{:T(128)}, f32[2,1024,4]{1,2,0:T(4,128)S(1)}, f32[2,4,1024]{2,1,0:T(4,128)S(1)}) all-reduce(f32[]{:T(128)S(6)} %div.95, f32[2,1024,4]{1,2,0:T(4,128)S(1)} %convolution_bitcast_fusion.1, f32[2,4,1024]{2,1,0:T(4,128)S(1)} %fusion.52), channel_id=1, replica_groups=mesh['dp'=8,'tensor'=4] {'dp','tensor'}, use_global_device_ids=true, to_apply=%region_21.22 | all-reduce | flops 16385 | bytes 131080 | tf_op jit(solution)/shard_map/psum | solution.py:284
  347.9 1.8 multiply_reduce_fusion.4
  349.7 1.8 fusion.84
  351.5 3.0 divide_convert_fusion.12
  357.7 17.1 %all-gather.6.cloned.1.call-done = bf16[1024,1024]{1,0:T(8,128)(2,1)} async-done(((bf16[256,1024]{1,0:T(8,128)(2,1)}), bf16[1024,1024]{1,0:T(8,128)(2,1)}) %all-gather.6.cloned.1.call-update) | async-done | bytes 2097168 | tf_op jit(solution)/shard_map/all_gather | solution.py:220
  374.8 37.6 %all-gather.8.cloned.1.call-done = bf16[1024,1024]{1,0:T(8,128)(2,1)} async-done(((bf16[256,1024]{1,0:T(8,128)(2,1)}), bf16[1024,1024]{1,0:T(8,128)(2,1)}) %all-gather.8.cloned.1.call-update) | async-done | bytes 2097168 | tf_op jit(solution)/shard_map/all_gather | solution.py:289
  412.4 3.2 copy.63
  415.7 1.3 copy.64
  (136 shorter events, 11.9 us)
Async XLA Ops:
  7.2 115.8 %copy-start = (bf16[1024,1024]{1,0:T(8,128)(2,1)S(1)}, bf16[1024,1024]{1,0:T(8,128)(2,1)}, u32[]{:S(2)}) copy-start(bf16[1024,1024]{1,0:T(8,128)(2,1)} %param.26) | copy-start | bytes 6291460
  7.2 77.5 %reduce-scatter.5.cloned.1.call-start = ((), (), s32[]{:S(2)}) async-start(), calls=%async_computation.4 | async-start | bytes 2621440 | tf_op jit(solution)/shard_map/reduce_scatter | solution.py:201
  9.2 8.0 %copy-start.26 = (f32[2,1024,4]{1,2,0:T(4,128)S(1)}, f32[2,1024,4]{1,2,0:T(4,128)}, u32[]{:S(2)}) copy-start(f32[2,1024,4]{1,2,0:T(4,128)} %param.28) | copy-start | bytes 98308
  11.2 6.7 %copy-start.29 = (f32[2,4,1024]{2,1,0:T(4,128)S(1)}, f32[2,4,1024]{2,1,0:T(4,128)}, u32[]{:S(2)}) copy-start(f32[2,4,1024]{2,1,0:T(4,128)} %param.29) | copy-start | bytes 98308
  15.9 1.3 copy-start.6
  17.9 1.7 copy-start.7
  17.9 2.4 copy-start.35
  23.3 1.6 copy-start.34
  31.4 3.2 copy-start.14
  31.4 3.2 copy-start.18
  31.4 3.2 copy-start.21
  34.6 4.2 copy-start.2
  36.6 5.9 %copy-start.3 = (f32[4,512,1024]{2,1,0:T(8,128)}, f32[4,512,1024]{2,1,0:T(8,128)S(1)}, u32[]{:S(2)}) copy-start(f32[4,512,1024]{2,1,0:T(8,128)S(1)} %get-tuple-element.55) | copy-start | bytes 25165828
  36.6 2.0 copy-start.13
  38.8 3.7 copy-start.11
  42.5 2.0 copy-start.24
  46.6 76.3 %all-gather.4.cloned.1.call-start = ((), (), s32[]{:S(2)}) async-start(), calls=%async_computation.5 | async-start | bytes 2621440 | tf_op jit(solution)/shard_map/all_gather | solution.py:209
  50.7 37.7 %copy-start.37 = (s32[8]{0:T(128)S(1)}, s32[8]{0:T(128)}, u32[]{:S(2)}) copy-start(s32[8]{0:T(128)} %param.20) | copy-start | bytes 100
  87.6 86.0 %reduce-scatter.9.cloned.1.call-start = ((), (), s32[]{:S(2)}) async-start(), calls=%async_computation.8 | async-start | bytes 2621440 | tf_op jit(solution)/shard_map/reduce_scatter | solution.py:225
  89.7 39.2 %copy-start.36 = (f32[1024]{0:T(1024)S(1)}, f32[1024]{0:T(1024)}, u32[]{:S(2)}) copy-start(f32[1024]{0:T(1024)} %param.23) | copy-start | bytes 12292
  138.3 7.5 %copy-start.16 = (bf16[1,1024,1024]{2,1,0:T(8,128)(2,1)S(1)}, bf16[1,1024,1024]{2,1,0:T(8,128)(2,1)}, u32[]{:S(2)}) copy-start(bf16[1,1024,1024]{2,1,0:T(8,128)(2,1)} %param.18) | copy-start | bytes 6291460
  138.3 73.4 %reduce-scatter.7.cloned.1.call-start = ((), (), s32[]{:S(2)}) async-start(), calls=%async_computation.6 | async-start | bytes 2621440 | tf_op jit(solution)/shard_map/reduce_scatter | solution.py:216
  145.5 202.4 %reduce-scatter.11.cloned.1.call-start = ((), (), s32[]{:S(2)}) async-start(), calls=%async_computation.9 | async-start | bytes 2621440 | tf_op jit(solution)/shard_map/reduce_scatter | solution.py:278
  214.1 45.2 %copy-start.9 = (f32[256,1024]{1,0:T(8,128)}, f32[256,1024]{1,0:T(8,128)S(1)}, u32[]{:S(2)}) copy-start(f32[256,1024]{1,0:T(8,128)S(1)} %get-tuple-element.30) | copy-start | bytes 3145732
  214.1 45.2 %copy-start.25 = (bf16[256,1024]{1,0:T(8,128)(2,1)S(1)}, bf16[256,1024]{1,0:T(8,128)(2,1)}, u32[]{:S(2)}) copy-start(bf16[256,1024]{1,0:T(8,128)(2,1)} %param.25) | copy-start | bytes 1572868
  217.9 14.4 %collective-permute-start = (bf16[256,1024]{1,0:T(8,128)(2,1)S(1)}, bf16[256,1024]{1,0:T(8,128)(2,1)S(1)}, u32[]{:S(2)}, u32[]{:S(2)}) collective-permute-start(bf16[256,1024]{1,0:T(8,128)(2,1)S(1)} %get-tuple-element.28), channel_id=1, source_target_pairs={{0,1},{1,2},{2,3},{3,0},{4,5},{5,6},{6,7},{7,4},{8,9},{9,10},{10,1... | collective-permute-start | bytes 1572872 | tf_op jit(solution)/shard_map/ppermute | solution.py:23
  232.3 13.5 %collective-permute-start.1 = (bf16[256,1024]{1,0:T(8,128)(2,1)S(1)}, bf16[256,1024]{1,0:T(8,128)(2,1)S(1)}, u32[]{:S(2)}, u32[]{:S(2)}) collective-permute-start(bf16[256,1024]{1,0:T(8,128)(2,1)S(1)} %collective-permute-done), channel_id=1, source_target_pairs={{0,1},{1,2},{2,3},{3,0},{4,5},{5,6},{6,7},{7,4},{8,9},{9,10},{10,1... | collective-permute-start | bytes 1572872 | tf_op jit(solution)/shard_map/ppermute | solution.py:23
  245.8 12.7 %collective-permute-start.2 = (bf16[256,1024]{1,0:T(8,128)(2,1)S(1)}, bf16[256,1024]{1,0:T(8,128)(2,1)S(1)}, u32[]{:S(2)}, u32[]{:S(2)}) collective-permute-start(bf16[256,1024]{1,0:T(8,128)(2,1)S(1)} %collective-permute-done.1), channel_id=1, source_target_pairs={{0,1},{1,2},{2,3},{3,0},{4,5},{5,6},{6,7},{7,4},{8,9},{9,10},{10,1... | collective-permute-start | bytes 1572872 | tf_op jit(solution)/shard_map/ppermute | solution.py:23
  259.3 7.5 %slice-start = ((s8[8388608]{0:T(1024)(128)(4,1)}), s8[4194304]{0:T(1024)(128)(4,1)S(1)}, s32[]{:S(2)}) async-start(s8[8388608]{0:T(1024)(128)(4,1)} %bitcast.151), calls=%async_computation.11 | async-start | bytes 8388608
  261.8 5.0 %slice-start.1 = ((s8[8388608]{0:T(1024)(128)(4,1)}), s8[4194304]{0:T(1024)(128)(4,1)S(1)}, s32[]{:S(2)}) async-start(s8[8388608]{0:T(1024)(128)(4,1)} %bitcast.151), calls=%async_computation.12 | async-start | bytes 8388608
  261.8 5.0 %copy-start.12 = (bf16[4,1024,64]{1,2,0:T(8,128)(2,1)S(1)}, bf16[4,1024,64]{1,2,0:T(8,128)(2,1)}, u32[]{:S(2)}) copy-start(bf16[4,1024,64]{1,2,0:T(8,128)(2,1)} %copy-done.11) | copy-start | bytes 1572868
  261.8 9.4 %slice-start.2 = ((s8[8388608]{0:T(1024)(128)(4,1)}), s8[4194304]{0:T(1024)(128)(4,1)S(1)}, s32[]{:S(2)}) async-start(s8[8388608]{0:T(1024)(128)(4,1)} %bitcast.153), calls=%async_computation.13 | async-start | bytes 8388608
  266.9 4.3 %slice-start.3 = ((s8[8388608]{0:T(1024)(128)(4,1)}), s8[4194304]{0:T(1024)(128)(4,1)S(1)}, s32[]{:S(2)}) async-start(s8[8388608]{0:T(1024)(128)(4,1)} %bitcast.153), calls=%async_computation.14 | async-start | bytes 8388608
  273.8 1.8 copy-start.19
  275.6 1.5 copy-start.15
  279.8 16.0 %copy-start.22 = (bf16[1,1024,256]{2,1,0:T(8,128)(2,1)}, bf16[1,1024,256]{2,1,0:T(8,128)(2,1)S(1)}, u32[]{:S(2)}) copy-start(bf16[1,1024,256]{2,1,0:T(8,128)(2,1)S(1)} %copy.36) | copy-start | bytes 1572868
  279.9 8.9 %copy-start.20 = (bf16[4,1024,64]{1,0,2:T(4,128)(2,1)S(1)}, bf16[4,1024,64]{1,0,2:T(4,128)(2,1)}, u32[]{:S(2)}) copy-start(bf16[4,1024,64]{1,0,2:T(4,128)(2,1)} %reshape.355) | copy-start | bytes 1572868
  286.8 2.0 copy-start.4
  290.5 5.4 %copy-start.23 = (bf16[1,1024,256]{2,1,0:T(8,128)(2,1)}, bf16[1,1024,256]{2,1,0:T(8,128)(2,1)S(1)}, u32[]{:S(2)}) copy-start(bf16[1,1024,256]{2,1,0:T(8,128)(2,1)S(1)} %copy.34) | copy-start | bytes 1572868
  290.5 4.2 %copy-start.5 = (bf16[4,512,1024]{2,1,0:T(8,128)(2,1)S(1)}, bf16[4,512,1024]{2,1,0:T(8,128)(2,1)}, u32[]{:S(2)}) copy-start(bf16[4,512,1024]{2,1,0:T(8,128)(2,1)} %copy-done.4) | copy-start | bytes 12582916
  301.7 3.8 copy-start.8
  301.7 73.1 %all-gather.6.cloned.1.call-start = ((), (), s32[]{:S(2)}) async-start(), calls=%async_computation.7 | async-start | bytes 2621440 | tf_op jit(solution)/shard_map/all_gather | solution.py:220
  301.7 49.7 %copy-start.10 = (f32[256,1024]{1,0:T(8,128)S(1)}, f32[256,1024]{1,0:T(8,128)}, u32[]{:S(2)}) copy-start(f32[256,1024]{1,0:T(8,128)} %copy-done.9) | copy-start | bytes 3145732
  302.3 110.2 %all-gather.8.cloned.1.call-start = ((), (), s32[]{:S(2)}) async-start(), calls=%async_computation.10 | async-start | bytes 2621440 | tf_op jit(solution)/shard_map/all_gather | solution.py:289
  306.4 48.7 %copy-start.32 = (f32[2,1024,4]{1,2,0:T(4,128)S(1)}, f32[2,1024,4]{1,2,0:T(4,128)}, u32[]{:S(2)}) copy-start(f32[2,1024,4]{1,2,0:T(4,128)} %param.30) | copy-start | bytes 98308
  306.4 49.4 %copy-start.30 = (f32[2,1024,4]{1,2,0:T(4,128)S(1)}, f32[2,1024,4]{1,2,0:T(4,128)}, u32[]{:S(2)}) copy-start(f32[2,1024,4]{1,2,0:T(4,128)} %param.32) | copy-start | bytes 98308
  306.5 50.0 %copy-start.33 = (f32[2,4,1024]{2,1,0:T(4,128)S(1)}, f32[2,4,1024]{2,1,0:T(4,128)}, u32[]{:S(2)}) copy-start(f32[2,4,1024]{2,1,0:T(4,128)} %param.31) | copy-start | bytes 98308
  347.9 9.2 %copy-start.31 = (f32[2,4,1024]{2,1,0:T(4,128)S(1)}, f32[2,4,1024]{2,1,0:T(4,128)}, u32[]{:S(2)}) copy-start(f32[2,4,1024]{2,1,0:T(4,128)} %param.33) | copy-start | bytes 98308
  355.8 61.2 %copy-start.27 = (f32[2,1024,4]{1,2,0:T(4,128)}, f32[2,1024,4]{1,2,0:T(4,128)S(1)}, u32[]{:S(2)}) copy-start(f32[2,1024,4]{1,2,0:T(4,128)S(1)} %get-tuple-element.78) | copy-start | bytes 98308
  357.1 59.9 %copy-start.28 = (f32[2,4,1024]{2,1,0:T(4,128)}, f32[2,4,1024]{2,1,0:T(4,128)S(1)}, u32[]{:S(2)}) copy-start(f32[2,4,1024]{2,1,0:T(4,128)S(1)} %get-tuple-element.79) | copy-start | bytes 98308
  412.4 3.2 copy-start.17
  412.4 4.6 %copy-start.1 = (bf16[1024,1024]{1,0:T(8,128)(2,1)S(1)}, bf16[1024,1024]{1,0:T(8,128)(2,1)}, u32[]{:S(2)}) copy-start(bf16[1024,1024]{1,0:T(8,128)(2,1)} %param.26) | copy-start | bytes 6291460
Sparse Core Ops, SparseCore 0:
  46.7 37.9 reduce-scatter.4
  87.8 35.1 all-gather.3
  138.4 35.1 reduce-scatter.8
  176.5 35.1 reduce-scatter.6
  301.8 36.0 reduce-scatter.10
  339.6 35.1 all-gather.5
  377.2 35.1 all-gather.7
